TPU v7x, 32 devices: a whole 2x2x4 slice. The times are simulated.
32 devices in a mesh: dp: 8 (over y, x, core), ctx: 4 (over z).
Axes of the slice: x: 2, y: 2, z: 4, core: 2. Of those that a mesh axis runs over, the one named last changes fastest.
Arguments:
- frames: bfloat16 [8192, 1024], P(('dp', 'ctx')), parts along dimension 0, may hold values from -20 to 20
- tile_source: int32 [512], P('dp'), parts along dimension 0, may hold values from 0 to 63, as said below
- tile_utt: int32 [512], P('dp'), parts along dimension 0, may hold values from 0 to 3, never falling along the last dimension, each value on 1 to 33 neighbouring positions
- query_weight: bfloat16 [1024, 512], replicated, may hold values from -1.625 to 1.625
- key_weight: bfloat16 [1024, 512], replicated, may hold values from -0.1875 to 0.1875
- value_weight: bfloat16 [1024, 512], replicated, may hold values from -0.1875 to 0.1875
- output_weight: bfloat16 [512, 1024], replicated, may hold values from -1.5 to 1.5
- depth_weight: float32 [31, 1024], replicated, may hold values from -1 to 1
- bn_scale: float32 [1024], replicated, may hold values from 0.5 to 2
- bn_shift: float32 [1024], replicated, may hold values from -3 to 3
Outputs:
- encoded: bfloat16 [8192, 1024], P(('dp', 'ctx')), parts along dimension 0
There are 8 independent parts, one for each index of `dp`. A program takes and returns all parts, laid end to end along the dimension named above; an argument that names none is the same for every part. Nothing has to cross between parts.
Inputs may be any that keep to these rules, and one draw needn't show every extreme that they name: `tile_source`: A permutation of the tiles of a part. The tiles that one shard receives come at most 4 from any one shard, and exactly 4 from some shard; for one tile position within a shard, the sources over all shards lie on distinct shards. `tile_utt`: never falls along the tiles; each of the 4 utterances holds 1 to 33 tiles, one exactly 33.
All inputs are finite; a program needn't handle non-finite values.
Results may differ from a plain program's by a relative error of at most 0.0068.
Values may be sent and summed in bfloat16 or wider, within the bound.
No kernel may reach another device: no remote copies, remote signals or barrier semaphores. Data moves between devices by JAX's collectives and lax.ppermute only.
A program may use at most 64 MiB of HBM per device.

v0:
```python
import math
import jax
import jax.numpy as jnp
from jax import lax
from jax.sharding import PartitionSpec as P

HEADS = 4
HEAD_DIM = 128
KERNEL = 31
TILE = 16
NEGATIVE = -1e30


def extended_2(block, sides, width):
    for axis, dim in sides:
        count = lax.axis_size(axis)
        forward = [(i, i + 1) for i in range(count - 1)]
        backward = [(target, source) for source, target in forward]
        low = lax.ppermute(
            lax.slice_in_dim(block, block.shape[dim] - width, None, axis=dim), axis, forward
        )
        high = lax.ppermute(lax.slice_in_dim(block, 0, width, axis=dim), axis, backward)
        block = jnp.concatenate([low, block, high], axis=dim)
    return block


def layer_norm(rows):
    values = rows.astype(jnp.float32)
    center = values - jnp.mean(values, axis=-1, keepdims=True)
    spread = jnp.mean(center * center, axis=-1, keepdims=True)
    return center * lax.rsqrt(spread + 1e-05)


def local_utt(row_utt, first_row, rows_here, total_rows):
    positions = first_row + jnp.arange(rows_here, dtype=jnp.int32)
    inside = (positions >= 0) & (positions < total_rows)
    picked = jnp.take(row_utt, jnp.clip(positions, 0, total_rows - 1), axis=0)
    return jnp.where(inside, picked, -1)


def attend(carried, key_block, value_block, key_utt, queries, query_utt, score_scale):
    weighted, running_max, running_sum = carried
    scores = (
        jnp.einsum("qhd,khd->hqk", queries, key_block, preferred_element_type=jnp.float32)
        * score_scale
    )
    allowed = (query_utt[:, None] == key_utt[None, :])[None]
    block_max = jnp.max(jnp.where(allowed, scores, NEGATIVE), axis=-1, keepdims=True)
    new_max = jnp.maximum(running_max, block_max)
    factor = jnp.exp(running_max - new_max)
    weights = jnp.where(allowed, jnp.exp(scores - new_max), 0.0)
    running_sum = running_sum * factor + jnp.sum(weights, axis=-1, keepdims=True)
    weighted = weighted * factor + jnp.einsum(
        "hqk,khd->hqd",
        weights.astype(jnp.bfloat16),
        value_block,
        preferred_element_type=jnp.float32,
    )
    return (weighted, new_max, running_sum)


def pick_block(rows_here, rows_dev):
    shard_count = rows_here // rows_dev
    group_limit = max(1, 1024 // rows_dev)
    return rows_dev * max(
        [
            grouping
            for grouping in range(1, shard_count + 1)
            if shard_count % grouping == 0 and grouping <= group_limit
        ]
    )


def per_device(
    frames,
    tile_source,
    tile_utt,
    query_weight,
    key_weight,
    value_weight,
    output_weight,
    depth_weight,
    bn_scale,
    bn_shift,
):
    shard_count = lax.axis_size("ctx")
    my_index = lax.axis_index("ctx")
    rows_dev, feature_width = frames.shape
    tiles_dev = rows_dev // TILE
    tile_total = tiles_dev * shard_count
    total_rows = tile_total * TILE
    slot_count = (tiles_dev + shard_count - 1) // shard_count
    positions = jnp.arange(tile_total, dtype=jnp.int32)
    source_dev = tile_source // tiles_dev
    source_slot = tile_source % tiles_dev
    dest_dev = positions // tiles_dev
    earlier = (
        (dest_dev[:, None] == dest_dev[None, :])
        & (source_dev[:, None] == source_dev[None, :])
        & (positions[None, :] < positions[:, None])
    )
    arrival_rank = jnp.sum(earlier.astype(jnp.int32), axis=1)
    shards = jnp.arange(shard_count, dtype=jnp.int32)
    places = jnp.arange(slot_count, dtype=jnp.int32)
    matches = (
        (source_dev[None, None, :] == my_index)
        & (dest_dev[None, None, :] == shards[:, None, None])
        & (arrival_rank[None, None, :] == places[None, :, None])
    )
    chosen = jnp.sum(jnp.where(matches, source_slot[None, None, :], 0), axis=2).reshape(-1)
    filled = jnp.any(matches, axis=2).reshape(-1)
    tile_rows = frames.reshape(tiles_dev, TILE, feature_width)
    outgoing = jnp.where(
        filled[:, None, None], jnp.take(tile_rows, chosen, axis=0), jnp.zeros((), frames.dtype)
    )
    outgoing = outgoing.reshape(shard_count, slot_count, TILE, feature_width)
    arrived = lax.all_to_all(outgoing, "ctx", split_axis=0, concat_axis=0, tiled=True)
    mine_source = lax.dynamic_slice_in_dim(source_dev, my_index * tiles_dev, tiles_dev)
    mine_rank = lax.dynamic_slice_in_dim(arrival_rank, my_index * tiles_dev, tiles_dev)
    grouped = jnp.take(
        arrived.reshape(shard_count * slot_count, TILE, feature_width),
        mine_source * slot_count + mine_rank,
        axis=0,
    ).reshape(rows_dev, feature_width)
    normed = layer_norm(grouped).astype(jnp.bfloat16)
    queries = (
        jnp.dot(normed, query_weight, preferred_element_type=jnp.float32)
        .astype(jnp.bfloat16)
        .reshape(rows_dev, HEADS, HEAD_DIM)
    )
    key_rows = jnp.dot(normed, key_weight, preferred_element_type=jnp.float32).astype(jnp.bfloat16)
    value_rows = jnp.dot(normed, value_weight, preferred_element_type=jnp.float32).astype(
        jnp.bfloat16
    )
    key_value = jnp.stack([key_rows, value_rows])
    row_utt = jnp.repeat(tile_utt, TILE)
    query_utt = lax.dynamic_slice_in_dim(row_utt, my_index * rows_dev, rows_dev)
    score_scale = 1.0 / math.sqrt(HEAD_DIM)
    start_state = (
        jnp.zeros((HEADS, rows_dev, HEAD_DIM), jnp.float32),
        jnp.full((HEADS, rows_dev, 1), NEGATIVE, jnp.float32),
        jnp.zeros((HEADS, rows_dev, 1), jnp.float32),
    )

    def block_update(carried, block_pair, key_utt):
        rows_here = block_pair.shape[1]
        key_block = block_pair[0].reshape(rows_here, HEADS, HEAD_DIM)
        value_block = block_pair[1].reshape(rows_here, HEADS, HEAD_DIM)
        return attend(carried, key_block, value_block, key_utt, queries, query_utt, score_scale)

    fetched = lax.all_gather(key_value, "ctx", axis=1, tiled=True)
    rows_here = fetched.shape[1]
    block_rows = pick_block(rows_here, rows_dev)

    def one_block(block_index, inner):
        section = lax.dynamic_slice_in_dim(fetched, block_index * block_rows, block_rows, 1)
        key_utt = local_utt(row_utt, block_index * block_rows, block_rows, total_rows)
        return block_update(inner, section, key_utt)

    carried = lax.fori_loop(0, rows_here // block_rows, one_block, start_state)
    weighted, running_max, running_sum = carried
    attended = (
        jnp.transpose(weighted / running_sum, (1, 0, 2))
        .reshape(rows_dev, HEADS * HEAD_DIM)
        .astype(jnp.bfloat16)
    )
    residual = (
        grouped.astype(jnp.float32)
        + jnp.dot(attended, output_weight, preferred_element_type=jnp.float32)
    ).astype(jnp.bfloat16)
    shaped = layer_norm(residual).astype(jnp.bfloat16)
    margin = (KERNEL - 1) // 2
    extended = extended_2(shaped, (("ctx", 0),), margin).astype(jnp.float32)
    extended_utt = local_utt(
        row_utt, my_index * rows_dev - margin, rows_dev + 2 * margin, total_rows
    )
    convolved = jnp.zeros((rows_dev, feature_width), jnp.float32)
    for offset in range(KERNEL):
        aligned = (extended_utt[offset : offset + rows_dev] == query_utt)[:, None]
        convolved = (
            convolved
            + jnp.where(aligned, extended[offset : offset + rows_dev], 0.0) * depth_weight[offset]
        )
    activation = convolved * bn_scale + bn_shift
    return (residual.astype(jnp.float32) + activation * jax.nn.sigmoid(activation)).astype(
        jnp.bfloat16
    )


def solution(mesh):
    return jax.shard_map(
        per_device,
        mesh=mesh,
        in_specs=(P(("dp", "ctx"), None), P("dp"), P("dp"), P(), P(), P(), P(), P(), P(), P()),
        out_specs=P(("dp", "ctx"), None),
        check_vma=False,
    )
```

profile of v0, /device:TPU:0, one launch (start us, length us, event | category | flops | bytes accessed | tf_op | source)
XLA Modules:
  0.0 121.9 jit_solution(12822432287140586318)
XLA Ops:
  6.5 0.8 and_select_fusion.1
  7.4 0.7 broadcast_compare_fusion.1
  8.7 1.6 %gather_fusion.2 = bf16[16,16,1024]{2,1,0:T(8,128)(2,1)S(1)} fusion(bf16[16,16,1024]{2,1,0:T(8,128)(2,1)} %bitcast.80, s32[1024]{0:T(1024)S(1)} %pad_clamp_fusion.2), kind=kCustom, calls=%fused_computation.clone | custom fusion | bytes 1048640 | tf_op jit(solution)/shard_map/jit(_take)/gather | solution.py:114
  10.4 0.9 select_select_fusion
  11.3 6.3 %all-to-all-start = ((bf16[4,4,16,1024]{3,2,1,0:T(8,128)(2,1)}), bf16[4,4,16,1024]{3,2,1,0:T(8,128)(2,1)S(1)}, u32[]{:S(2)}, u32[]{:S(2)}) async-start(bf16[4,4,16,1024]{3,2,1,0:T(8,128)(2,1)} %bitcast.1), calls=%async_computation | async-start | bytes 1048576 | tf_op jit(solution)/shard_map/all_to_all | solution.py:117
  17.7 14.4 %all-to-all-done = bf16[4,4,16,1024]{3,2,1,0:T(8,128)(2,1)S(1)} async-done(((bf16[4,4,16,1024]{3,2,1,0:T(8,128)(2,1)}), bf16[4,4,16,1024]{3,2,1,0:T(8,128)(2,1)S(1)}, u32[]{:S(2)}, u32[]{:S(2)}) %all-to-all-start) | async-done | bytes 524320 | tf_op jit(solution)/shard_map/all_to_all | solution.py:117
  32.1 0.6 gather_fusion.3
  32.7 0.2 convert_reduce_fusion.1
  33.0 0.3 multiply_reduce_fusion
  33.7 0.4 fusion.18
  34.2 1.7 %fusion.19 = bf16[1,256,512]{2,1,0:T(8,128)(2,1)S(1)} fusion(bf16[256,1024]{1,0:T(8,128)(2,1)S(1)} %fusion.87, bf16[1024,512]{1,0:T(8,128)(2,1)} %param.17), kind=kOutput, calls=%fused_computation.27 | convolution fusion | flops 268566528 | bytes 1835008 | tf_op jit(solution)/shard_map/dot_general | solution.py:132
  35.9 0.8 pad_maximum_fusion
  36.9 1.7 %gather_fusion.1 = s32[286]{0:T(512)S(1)} fusion(s32[1024]{0:T(1024)S(1)} %reshape.320, s32[1024]{0:T(1024)S(1)} %pad_clamp_fusion), kind=kCustom, calls=%fused_computation.3 | custom fusion | bytes 3432 | tf_op jit(solution)/shard_map/jit(_take)/gather | solution.py:37
  38.6 4.5 %gather_fusion = s32[1024]{0:T(1024)S(1)} fusion(s32[1024]{0:T(1024)S(1)} %reshape.320, s32[1024]{0:T(1024)S(1)} %broadcast_clamp_fusion), kind=kCustom, calls=%fused_computation.2 | custom fusion | bytes 12288 | tf_op jit(solution)/shard_map/while/body/eval_jaxpr/jit(_take)/gather | solution.py:37
  43.2 0.6 slice_compare_fusion.30
  43.8 0.7 slice_compare_fusion.29
  44.9 1.2 fusion.17
  46.2 35.4 %all-gather.2.cloned.1.call-done = bf16[2,1024,512]{2,1,0:T(8,128)(2,1)} async-done(((bf16[2,256,512]{2,1,0:T(8,128)(2,1)}), bf16[2,1024,512]{2,1,0:T(8,128)(2,1)}) %all-gather.2.cloned.1.call-update) | async-done | bytes 2097168 | tf_op jit(solution)/shard_map/all_gather | solution.py:151
  81.7 3.0 %fusion.111 = (bf16[1,1024,512]{2,1,0:T(8,128)(2,1)}, bf16[1,1024,512]{2,1,0:T(8,128)(2,1)}) fusion(bf16[2,1024,512]{2,1,0:T(8,128)(2,1)} %all-gather.2.cloned.1.call-done), kind=kLoop, calls=%fused_computation.224 | loop fusion | bytes 4194304 | tf_op jit(solution)/shard_map/while/body/eval_jaxpr/slice | solution.py:147
  84.7 2.2 %squeeze.8 = bf16[1024,4,128]{2,1,0:T(4,128)(2,1)} reshape(bf16[1,1024,512]{2,1,0:T(8,128)(2,1)} %get-tuple-element.38) | data formatting | bytes 2097152 | tf_op jit(solution)/shard_map/while/body/eval_jaxpr/reshape;while/body/eval_jaxpr/squeeze | solution.py:147
  86.8 2.3 %select_reduce_fusion = (f32[4,256]{1,0:T(4,128)S(1)}, f32[4,256,1024]{2,1,0:T(8,128)S(1)}) fusion(pred[256,1024]{1,0:T(8,128)(4,1)S(1)} %broadcast_compare_fusion, bf16[1024,4,128]{2,1,0:T(4,128)(2,1)} %squeeze.8, bf16[32,4,8,128]{3,2,1,0:T(8,128)(2,1)S(1)} %copy-done.4), kind=kOutput, calls=%fused_computation.5 | convolution fusion | flops 271580160 | bytes 5771264 | tf_op jit(solution)/shard_map/while/body/eval_jaxpr/qhd,khd->hqk/dot_general | solution.py:44
  89.2 1.9 %copy-done.1 = f32[4,256,1024]{2,1,0:T(8,128)} copy-done((f32[4,256,1024]{2,1,0:T(8,128)}, f32[4,256,1024]{2,1,0:T(8,128)S(1)}, u32[]{:S(2)}) %copy-start.1) | copy-done | bytes 4194328
  91.1 1.4 %fusion = f32[4,256]{1,0:T(4,128)S(1)} fusion(f32[4,256,1024]{2,1,0:T(8,128)S(1)} %get-tuple-element.107, f32[4,256]{1,0:T(4,128)S(1)} %get-tuple-element.75, pred[256,1024]{1,0:T(8,128)(4,1)S(1)} %broadcast_compare_fusion), kind=kLoop, calls=%fused_computation.6 | loop fusion | flops 4193280 | bytes 4464640 | tf_op jit(solution)/shard_map/while/body/eval_jaxpr/reduce_sum | solution.py:52
  92.5 2.3 %copy.20 = bf16[1,1024,512]{1,2,0:T(8,128)(2,1)} copy(bf16[1,1024,512]{2,1,0:T(8,128)(2,1)} %get-tuple-element.40) | data formatting | bytes 2097152 | tf_op jit(solution)/shard_map/while/body/eval_jaxpr/reshape;while/body/eval_jaxpr/squeeze | solution.py:148
  94.8 3.6 %fusion.93 = bf16[256,4,128]{0,2,1:T(8,128)(2,1)S(1)} fusion(bf16[1024,4,128]{0,2,1:T(8,128)(2,1)} %bitcast.79, f32[4,256,1024]{2,1,0:T(8,128)} %copy-done.1, f32[4,256]{1,0:T(4,128)S(1)} %get-tuple-element.75, pred[256,1024]{1,0:T(8,128)(4,1)S(1)} %broadcast_compare_fusion, f32[256,4]{0,1:T(4,128)S(1)} %bitcast_add_fusion, f32[256,4]{0,1:T(4,128)S(1)} %get-tuple-element.74), kind=kOutput, calls=%fused_computation.132 | convolution fusion | flops 273022976 | bytes 5779456 | tf_op jit(solution)/shard_map/while/body/eval_jaxpr/hqk,khd->hqd/dot_general | solution.py:53
  98.6 0.5 convert_reduce_fusion
  99.2 0.3 fusion.20
  99.5 0.3 fusion.21
  99.8 2.1 %collective-permute-start = (bf16[15,1024]{1,0:T(8,128)(2,1)S(1)}, bf16[15,1024]{1,0:T(8,128)(2,1)S(1)}, u32[]{:S(2)}, u32[]{:S(2)}) collective-permute-start(bf16[15,1024]{1,0:T(8,128)(2,1)S(1)} %get-tuple-element.41), channel_id=1, source_target_pairs={{0,1},{1,2},{2,3},{4,5},{5,6},{6,7},{8,9},{9,10},{10,11},{12,13},{... | collective-permute-start | bytes 92168 | tf_op jit(solution)/shard_map/ppermute | solution.py:19
  101.9 1.3 %collective-permute-start.1 = (bf16[15,1024]{1,0:T(8,128)(2,1)S(1)}, bf16[15,1024]{1,0:T(8,128)(2,1)S(1)}, u32[]{:S(2)}, u32[]{:S(2)}) collective-permute-start(bf16[15,1024]{1,0:T(8,128)(2,1)S(1)} %get-tuple-element.42), channel_id=1, source_target_pairs={{1,0},{2,1},{3,2},{5,4},{6,5},{7,6},{9,8},{10,9},{11,10},{13,12},{... | collective-permute-start | bytes 92168 | tf_op jit(solution)/shard_map/ppermute | solution.py:22
  103.4 4.2 %collective-permute-done.1 = bf16[15,1024]{1,0:T(8,128)(2,1)S(1)} collective-permute-done((bf16[15,1024]{1,0:T(8,128)(2,1)S(1)}, bf16[15,1024]{1,0:T(8,128)(2,1)S(1)}, u32[]{:S(2)}, u32[]{:S(2)}) %collective-permute-start.1) | collective-permute-done | bytes 30752 | tf_op jit(solution)/shard_map/ppermute | solution.py:22
  108.0 7.0 %fusion.22 = bf16[256,1024]{1,0:T(8,128)(2,1)} fusion(bf16[256,1024]{1,0:T(8,128)(2,1)S(1)} %get-tuple-element.109, f32[286,1024]{1,0:T(8,128)S(1)} %maximum_convert_fusion, f32[1024]{0:T(1024)S(1)} %copy-done.6, f32[1024]{0:T(1024)S(1)} %copy-done.7, f32[1024]{0:T(1024)S(1)} %bitcast.92, f32[1024]{0:T(1024)S(1)} %bitcast.93, f32[1024]{0:T(1024)S(1)} %bitcast.95, ...), kind=kLoop, calls=%fused_computation.30 | loop fusion | flops 26476544 | bytes 33697536 | tf_op jit(solution)/shard_map/convert_element_type | solution.py:185
  (92 shorter events, 2.5 us)
Async XLA Ops:
  6.5 92.1 %copy-start = (bf16[512,1024]{1,0:T(8,128)(2,1)S(1)}, bf16[512,1024]{1,0:T(8,128)(2,1)}, u32[]{:S(2)}) copy-start(bf16[512,1024]{1,0:T(8,128)(2,1)} %param.18) | copy-start | bytes 3145732
  6.5 27.2 %copy-start.2 = (bf16[1024,512]{1,0:T(8,128)(2,1)S(1)}, bf16[1024,512]{1,0:T(8,128)(2,1)}, u32[]{:S(2)}) copy-start(bf16[1024,512]{1,0:T(8,128)(2,1)} %param.16) | copy-start | bytes 3145732
  11.3 20.8 %all-to-all-start = ((bf16[4,4,16,1024]{3,2,1,0:T(8,128)(2,1)}), bf16[4,4,16,1024]{3,2,1,0:T(8,128)(2,1)S(1)}, u32[]{:S(2)}, u32[]{:S(2)}) async-start(bf16[4,4,16,1024]{3,2,1,0:T(8,128)(2,1)} %bitcast.1), calls=%async_computation | async-start | bytes 1048576 | tf_op jit(solution)/shard_map/all_to_all | solution.py:117
  17.6 64.0 %all-gather.2.cloned.1.call-start = ((), (), s32[]{:S(2)}) async-start(), calls=%async_computation.1 | async-start | bytes 2621440 | tf_op jit(solution)/shard_map/all_gather | solution.py:151
  32.1 4.6 %copy-start.26 = (s32[64]{0:T(128)S(1)}, s32[64]{0:T(128)}, u32[]{:S(2)}) copy-start(s32[64]{0:T(128)} %param.14) | copy-start | bytes 772
  35.8 8.7 %copy-start.5 = (f32[31,1024]{1,0:T(8,128)S(1)}, f32[31,1024]{1,0:T(8,128)}, u32[]{:S(2)}) copy-start(f32[31,1024]{1,0:T(8,128)} %param.19) | copy-start | bytes 380932
  35.8 9.0 %copy-start.3 = (bf16[1024,512]{1,0:T(8,128)(2,1)S(1)}, bf16[1024,512]{1,0:T(8,128)(2,1)}, u32[]{:S(2)}) copy-start(bf16[1024,512]{1,0:T(8,128)(2,1)} %param.15) | copy-start | bytes 3145732
  46.1 40.8 %copy-start.4 = (bf16[32,4,8,128]{3,2,1,0:T(8,128)(2,1)S(1)}, bf16[32,4,8,128]{3,2,1,0:T(8,128)(2,1)}, u32[]{:S(2)}) copy-start(bf16[32,4,8,128]{3,2,1,0:T(8,128)(2,1)} %fusion.17) | copy-start | bytes 786436
  89.1 2.0 %copy-start.1 = (f32[4,256,1024]{2,1,0:T(8,128)}, f32[4,256,1024]{2,1,0:T(8,128)S(1)}, u32[]{:S(2)}) copy-start(f32[4,256,1024]{2,1,0:T(8,128)S(1)} %get-tuple-element.107) | copy-start | bytes 12582916
  98.4 9.4 %copy-start.6 = (f32[1024]{0:T(1024)S(1)}, f32[1024]{0:T(1024)}, u32[]{:S(2)}) copy-start(f32[1024]{0:T(1024)} %param.21) | copy-start | bytes 12292
  98.4 9.4 %copy-start.7 = (f32[1024]{0:T(1024)S(1)}, f32[1024]{0:T(1024)}, u32[]{:S(2)}) copy-start(f32[1024]{0:T(1024)} %param.20) | copy-start | bytes 12292
  98.4 9.4 %copy-start.8 = (pred[256]{0:T(512)(128)(4,1)S(1)}, pred[256]{0:T(512)(128)(4,1)}, u32[]{:S(2)}) copy-start(pred[256]{0:T(512)(128)(4,1)} %get-tuple-element.77) | copy-start | bytes 772
  98.4 9.4 %copy-start.9 = (pred[256]{0:T(512)(128)(4,1)S(1)}, pred[256]{0:T(512)(128)(4,1)}, u32[]{:S(2)}) copy-start(pred[256]{0:T(512)(128)(4,1)} %get-tuple-element.78) | copy-start | bytes 772
  98.4 9.4 %copy-start.10 = (pred[256]{0:T(512)(128)(4,1)S(1)}, pred[256]{0:T(512)(128)(4,1)}, u32[]{:S(2)}) copy-start(pred[256]{0:T(512)(128)(4,1)} %get-tuple-element.79) | copy-start | bytes 772
  98.5 9.4 %copy-start.11 = (pred[256]{0:T(512)(128)(4,1)S(1)}, pred[256]{0:T(512)(128)(4,1)}, u32[]{:S(2)}) copy-start(pred[256]{0:T(512)(128)(4,1)} %get-tuple-element.80) | copy-start | bytes 772
  98.5 9.4 %copy-start.12 = (pred[256]{0:T(512)(128)(4,1)S(1)}, pred[256]{0:T(512)(128)(4,1)}, u32[]{:S(2)}) copy-start(pred[256]{0:T(512)(128)(4,1)} %get-tuple-element.81) | copy-start | bytes 772
  98.5 9.4 %copy-start.13 = (pred[256]{0:T(512)(128)(4,1)S(1)}, pred[256]{0:T(512)(128)(4,1)}, u32[]{:S(2)}) copy-start(pred[256]{0:T(512)(128)(4,1)} %get-tuple-element.82) | copy-start | bytes 772
  98.5 9.4 %copy-start.14 = (pred[256]{0:T(512)(128)(4,1)S(1)}, pred[256]{0:T(512)(128)(4,1)}, u32[]{:S(2)}) copy-start(pred[256]{0:T(512)(128)(4,1)} %get-tuple-element.83) | copy-start | bytes 772
  98.5 9.4 %copy-start.15 = (pred[256]{0:T(512)(128)(4,1)S(1)}, pred[256]{0:T(512)(128)(4,1)}, u32[]{:S(2)}) copy-start(pred[256]{0:T(512)(128)(4,1)} %get-tuple-element.84) | copy-start | bytes 772
  98.5 9.4 %copy-start.16 = (pred[256]{0:T(512)(128)(4,1)S(1)}, pred[256]{0:T(512)(128)(4,1)}, u32[]{:S(2)}) copy-start(pred[256]{0:T(512)(128)(4,1)} %get-tuple-element.85) | copy-start | bytes 772
  98.5 9.4 %copy-start.17 = (pred[256]{0:T(512)(128)(4,1)S(1)}, pred[256]{0:T(512)(128)(4,1)}, u32[]{:S(2)}) copy-start(pred[256]{0:T(512)(128)(4,1)} %get-tuple-element.86) | copy-start | bytes 772
  98.5 9.4 %copy-start.18 = (pred[256]{0:T(512)(128)(4,1)S(1)}, pred[256]{0:T(512)(128)(4,1)}, u32[]{:S(2)}) copy-start(pred[256]{0:T(512)(128)(4,1)} %get-tuple-element.87) | copy-start | bytes 772
  98.5 9.4 %copy-start.19 = (pred[256]{0:T(512)(128)(4,1)S(1)}, pred[256]{0:T(512)(128)(4,1)}, u32[]{:S(2)}) copy-start(pred[256]{0:T(512)(128)(4,1)} %get-tuple-element.88) | copy-start | bytes 772
  98.5 9.4 %copy-start.20 = (pred[256]{0:T(512)(128)(4,1)S(1)}, pred[256]{0:T(512)(128)(4,1)}, u32[]{:S(2)}) copy-start(pred[256]{0:T(512)(128)(4,1)} %get-tuple-element.89) | copy-start | bytes 772
  98.6 9.4 %copy-start.21 = (pred[256]{0:T(512)(128)(4,1)S(1)}, pred[256]{0:T(512)(128)(4,1)}, u32[]{:S(2)}) copy-start(pred[256]{0:T(512)(128)(4,1)} %get-tuple-element.90) | copy-start | bytes 772
  98.6 9.4 %copy-start.22 = (pred[256]{0:T(512)(128)(4,1)S(1)}, pred[256]{0:T(512)(128)(4,1)}, u32[]{:S(2)}) copy-start(pred[256]{0:T(512)(128)(4,1)} %get-tuple-element.91) | copy-start | bytes 772
  98.6 9.4 %copy-start.23 = (pred[256]{0:T(512)(128)(4,1)S(1)}, pred[256]{0:T(512)(128)(4,1)}, u32[]{:S(2)}) copy-start(pred[256]{0:T(512)(128)(4,1)} %get-tuple-element.92) | copy-start | bytes 772
  98.6 9.4 %copy-start.24 = (pred[256]{0:T(512)(128)(4,1)S(1)}, pred[256]{0:T(512)(128)(4,1)}, u32[]{:S(2)}) copy-start(pred[256]{0:T(512)(128)(4,1)} %get-tuple-element.93) | copy-start | bytes 772
  98.6 9.4 %copy-start.25 = (pred[256]{0:T(512)(128)(4,1)S(1)}, pred[256]{0:T(512)(128)(4,1)}, u32[]{:S(2)}) copy-start(pred[256]{0:T(512)(128)(4,1)} %get-tuple-element.22) | copy-start | bytes 772
  99.8 3.7 %collective-permute-start = (bf16[15,1024]{1,0:T(8,128)(2,1)S(1)}, bf16[15,1024]{1,0:T(8,128)(2,1)S(1)}, u32[]{:S(2)}, u32[]{:S(2)}) collective-permute-start(bf16[15,1024]{1,0:T(8,128)(2,1)S(1)} %get-tuple-element.41), channel_id=1, source_target_pairs={{0,1},{1,2},{2,3},{4,5},{5,6},{6,7},{8,9},{9,10},{10,11},{12,13},{... | collective-permute-start | bytes 92168 | tf_op jit(solution)/shard_map/ppermute | solution.py:19
  101.9 5.8 %collective-permute-start.1 = (bf16[15,1024]{1,0:T(8,128)(2,1)S(1)}, bf16[15,1024]{1,0:T(8,128)(2,1)S(1)}, u32[]{:S(2)}, u32[]{:S(2)}) collective-permute-start(bf16[15,1024]{1,0:T(8,128)(2,1)S(1)} %get-tuple-element.42), channel_id=1, source_target_pairs={{1,0},{2,1},{3,2},{5,4},{6,5},{7,6},{9,8},{10,9},{11,10},{13,12},{... | collective-permute-start | bytes 92168 | tf_op jit(solution)/shard_map/ppermute | solution.py:22
Sparse Core Ops, SparseCore 0:
  36.8 44.7 all-gather.1
where the time goes:
time: 122 us
  waiting for transfers between devices  54.3 us (45%)
  local copies, waits for them, and re-layouts  18.6 us (15%)
  other arithmetic  15.6 us (13%)
  between operations  14 us (11%)
  starting transfers between devices  9.73 us (8%)
  matrix products  9.73 us (8%)
    all_gather x1, waiting for transfers between devices, per_device(): fetched = lax.all_gather(key_value, 'ctx', axis=1, tiled=True)  35.4 us
    all_to_all x1, waiting for transfers between devices, per_device(): lax.all_to_all(outgoing, 'ctx', split_axis=0, concat_axis=0, tiled=True)  14.4 us
    convert_element_type x1, other arithmetic, per_device(): (residual.astype(jnp.float32) + activation * jax.nn.sigmoid(activation))....  7.03 us
    all_to_all x1, starting transfers between devices, per_device(): lax.all_to_all(outgoing, 'ctx', split_axis=0, concat_axis=0, tiled=True)  6.35 us
    gather x2, local copies, waits for them, and re-layouts, local_utt(): picked = jnp.take(row_utt, jnp.clip(positions, 0, total_rows - 1), axis=0)  6.22 us
    ppermute x1, waiting for transfers between devices, extended_2(): lax.ppermute(lax.slice_in_dim(block, 0, width, axis=dim), axis, backward)  4.23 us
    dot_general x1, matrix products, attend(): jnp.einsum('hqk,khd->hqd', weights.astype(jnp.bfloat16), value_block, pre...  3.63 us
    slice x1, local copies, waits for them, and re-layouts, block_update(): key_block = block_pair[0].reshape(rows_here, HEADS, HEAD_DIM)  3.01 us
  transfers between devices with their start and end apart: 4, of which 4 were waited for; matrix products, arithmetic and copies ran while one was open for 8% of the time, Pallas kernels for 0%

commit v1 on v0

--- a/solution.py
+++ b/solution.py
@@ -148,7 +148,15 @@
         value_block = block_pair[1].reshape(rows_here, HEADS, HEAD_DIM)
         return attend(carried, key_block, value_block, key_utt, queries, query_utt, score_scale)
 
-    fetched = lax.all_gather(key_value, "ctx", axis=1, tiled=True)
+    count_2 = lax.axis_size("ctx")
+    current, blocks = (key_value, [key_value])
+    for _ in range(count_2 - 1):
+        current = lax.ppermute(
+            current, "ctx", [(i_2, (i_2 + 1) % count_2) for i_2 in range(count_2)]
+        )
+        blocks.insert(0, current)
+    flat = jnp.concatenate(blocks, axis=1)
+    fetched = jnp.roll(flat, (lax.axis_index("ctx") + 1) * key_value.shape[1], axis=1)
     rows_here = fetched.shape[1]
     block_rows = pick_block(rows_here, rows_dev)
 

time: 122 us -> 106 us (0.87)
  between operations: 14 us -> 0.94 us
  waiting for transfers between devices: 54.3 us -> 46.8 us
  other arithmetic: 15.6 us -> 18.3 us
    all_gather x1 -> x0, waiting for transfers between devices: 35.4 us -> none  [per_device(): fetched = lax.all_gather(key_value, 'ctx', axis=1, tiled=True)]
    ppermute x0 -> x3, waiting for transfers between devices: none -> 30.6 us  [per_device(): lax.ppermute(current, 'ctx', [(i_2, (i_2 + 1) % count_2) for i_2 in range...]
    unnamed x54 -> x96, local copies, waits for them, and re-layouts: 2.06 us -> 6.51 us
    slice x1, local copies, waits for them, and re-layouts: 3.01 us -> 0.17 us  [block_update(): key_block = block_pair[0].reshape(rows_here, HEADS, HEAD_DIM)]
    all_to_all x1, waiting for transfers between devices: 14.4 us -> 11.8 us  [per_device(): lax.all_to_all(outgoing, 'ctx', split_axis=0, concat_axis=0, tiled=True)]
    squeeze x1, local copies, waits for them, and re-layouts: 2.29 us -> 0.54 us  [block_update(): value_block = block_pair[1].reshape(rows_here, HEADS, HEAD_DIM)]
    convert_element_type x1, other arithmetic: 0.14 us -> 1.85 us  [per_device(): grouped.astype(jnp.float32)]
    slice x2, local copies, waits for them, and re-layouts: 0.1 us -> 1.34 us  [per_device(): depth_weight[offset]]
  transfers between devices with their start and end apart: 4 -> 6, of which waited for: 4 -> 6; matrix products, arithmetic and copies ran while one was open for 8% -> 14% of each run, Pallas kernels for 0% -> 0%
where the time goes in v1:
time: 106 us; the launch traced here: 105 us
  waiting for transfers between devices  46.8 us (44%)
  local copies, waits for them, and re-layouts  19.3 us (18%)
  other arithmetic  18.3 us (17%)
  matrix products  10.8 us (10%)
  starting transfers between devices  8.94 us (8%)
    ppermute x3, waiting for transfers between devices, per_device(): lax.ppermute(current, 'ctx', [(i_2, (i_2 + 1) % count_2) for i_2 in range...  30.6 us
    all_to_all x1, waiting for transfers between devices, per_device(): lax.all_to_all(outgoing, 'ctx', split_axis=0, concat_axis=0, tiled=True)  11.8 us
    convert_element_type x1, other arithmetic, per_device(): (residual.astype(jnp.float32) + activation * jax.nn.sigmoid(activation))....  7.95 us
    unnamed x96, local copies, waits for them, and re-layouts  6.51 us
    all_to_all x1, starting transfers between devices, per_device(): lax.all_to_all(outgoing, 'ctx', split_axis=0, concat_axis=0, tiled=True)  6.35 us
    gather x2, local copies, waits for them, and re-layouts, local_utt(): picked = jnp.take(row_utt, jnp.clip(positions, 0, total_rows - 1), axis=0)  6.22 us
    ppermute x1, waiting for transfers between devices, extended_2(): lax.ppermute(lax.slice_in_dim(block, 0, width, axis=dim), axis, backward)  4.23 us
    dot_general x1, matrix products, attend(): jnp.einsum('hqk,khd->hqd', weights.astype(jnp.bfloat16), value_block, pre...  3.41 us
  transfers between devices with their start and end apart: 6, of which 6 were waited for; matrix products, arithmetic and copies ran while one was open for 14% of the time, Pallas kernels for 0%

profile of v1, /device:TPU:0, one launch (start us, length us, event | category | flops | bytes accessed | tf_op | source)
XLA Modules:
  0.0 105.1 jit_solution(6335966125199071597)
XLA Ops:
  0.0 0.8 and_select_fusion.1
  0.8 0.7 broadcast_compare_fusion.1
  2.1 1.7 %gather_fusion.2 = bf16[16,16,1024]{2,1,0:T(8,128)(2,1)S(1)} fusion(bf16[16,16,1024]{2,1,0:T(8,128)(2,1)} %bitcast.80, s32[1024]{0:T(1024)S(1)} %pad_clamp_fusion.2), kind=kCustom, calls=%fused_computation.clone | custom fusion | bytes 1048640 | tf_op jit(solution)/shard_map/jit(_take)/gather | solution.py:114
  3.9 0.9 select_select_fusion
  4.8 6.3 %all-to-all-start = ((bf16[4,4,16,1024]{3,2,1,0:T(8,128)(2,1)}), bf16[4,4,16,1024]{3,2,1,0:T(8,128)(2,1)S(1)}, u32[]{:S(2)}, u32[]{:S(2)}) async-start(bf16[4,4,16,1024]{3,2,1,0:T(8,128)(2,1)} %bitcast.1), calls=%async_computation | async-start | bytes 1048576 | tf_op jit(solution)/shard_map/all_to_all | solution.py:117
  11.1 0.7 broadcast_in_dim.349
  12.0 1.7 %gather_fusion.1 = s32[286]{0:T(512)S(1)} fusion(s32[1024]{0:T(1024)S(1)} %reshape.320, s32[1024]{0:T(1024)S(1)} %get-tuple-element.112), kind=kCustom, calls=%fused_computation.3 | custom fusion | bytes 3432 | tf_op jit(solution)/shard_map/jit(_take)/gather | solution.py:37
  13.8 11.8 %all-to-all-done = bf16[4,4,16,1024]{3,2,1,0:T(8,128)(2,1)S(1)} async-done(((bf16[4,4,16,1024]{3,2,1,0:T(8,128)(2,1)}), bf16[4,4,16,1024]{3,2,1,0:T(8,128)(2,1)S(1)}, u32[]{:S(2)}, u32[]{:S(2)}) %all-to-all-start) | async-done | bytes 524320 | tf_op jit(solution)/shard_map/all_to_all | solution.py:117
  27.7 1.7 %fusion.19 = bf16[1,256,512]{2,1,0:T(8,128)(2,1)S(1)} fusion(bf16[256,1024]{1,0:T(8,128)(2,1)S(1)} %fusion.87, bf16[1024,512]{1,0:T(8,128)(2,1)} %param.17), kind=kOutput, calls=%fused_computation.27 | convolution fusion | flops 268566528 | bytes 1835008 | tf_op jit(solution)/shard_map/dot_general | solution.py:132
  29.4 0.8 pad_maximum_fusion
  30.2 4.5 %gather_fusion = s32[1024]{0:T(1024)S(1)} fusion(s32[1024]{0:T(1024)S(1)} %reshape.320, s32[1024]{0:T(1024)S(1)} %get-tuple-element.113), kind=kCustom, calls=%fused_computation.2 | custom fusion | bytes 12288 | tf_op jit(solution)/shard_map/while/body/eval_jaxpr/jit(_take)/gather | solution.py:37
  34.8 0.6 fusion.113
  35.4 9.7 %collective-permute-done = bf16[2,256,512]{2,1,0:T(8,128)(2,1)S(1)} collective-permute-done((bf16[2,256,512]{2,1,0:T(8,128)(2,1)}, bf16[2,256,512]{2,1,0:T(8,128)(2,1)S(1)}, u32[]{:S(2)}, u32[]{:S(2)}) %collective-permute-start) | collective-permute-done | bytes 524320 | tf_op jit(solution)/shard_map/ppermute | solution.py:154
  45.8 0.7 fusion.112
  46.7 12.4 %collective-permute-done.1 = bf16[2,256,512]{2,1,0:T(8,128)(2,1)} collective-permute-done((bf16[2,256,512]{2,1,0:T(8,128)(2,1)S(1)}, bf16[2,256,512]{2,1,0:T(8,128)(2,1)}, u32[]{:S(2)}, u32[]{:S(2)}) %collective-permute-start.1) | collective-permute-done | bytes 524320 | tf_op jit(solution)/shard_map/ppermute | solution.py:154
  59.1 0.7 slice_compare_fusion.29
  59.9 2.4 %fusion.17 = bf16[32,4,8,128]{3,2,1,0:T(8,128)(2,1)} fusion(bf16[256,1024]{1,0:T(8,128)(2,1)S(1)} %fusion.87, bf16[1024,512]{1,0:T(8,128)(2,1)} %param.15), kind=kOutput, calls=%fused_computation.25 | convolution fusion | flops 268566528 | bytes 1835008 | tf_op jit(solution)/shard_map/dot_general | solution.py:127
  62.2 1.9 %fusion.110 = f32[16,16,1024]{2,1,0:T(8,128)} fusion(bf16[16,16,1024]{2,1,0:T(8,128)(2,1)S(1)} %gather_fusion.3, pred[16]{0:T(512)(128)(4,1)} %copy-done.36), kind=kLoop, calls=%fused_computation.233 | loop fusion | flops 524288 | bytes 1572880 | tf_op jit(solution)/shard_map/convert_element_type | solution.py:176
  64.1 8.4 %collective-permute-done.2 = bf16[2,256,512]{2,1,0:T(8,128)(2,1)} collective-permute-done((bf16[2,256,512]{2,1,0:T(8,128)(2,1)}, bf16[2,256,512]{2,1,0:T(8,128)(2,1)}, u32[]{:S(2)}, u32[]{:S(2)}) %collective-permute-start.2) | collective-permute-done | bytes 524320 | tf_op jit(solution)/shard_map/ppermute | solution.py:154
  72.5 1.1 %constant_dynamic-update-slice_fusion.7 = bf16[2,2048,512]{2,1,0:T(8,128)(2,1)S(1)} fusion(bf16[2,256,512]{2,1,0:T(8,128)(2,1)} %collective-permute-done.2), kind=kLoop, calls=%fused_computation.152 | loop fusion | bytes 1048576
  73.5 1.1 %constant_dynamic-update-slice_fusion.6 = bf16[2,2048,512]{2,1,0:T(8,128)(2,1)S(1)} fusion(bf16[2,2048,512]{2,1,0:T(8,128)(2,1)S(1)} %constant_dynamic-update-slice_fusion.7, bf16[2,256,512]{2,1,0:T(8,128)(2,1)} %collective-permute-done.1), kind=kLoop, calls=%fused_computation.151 | loop fusion | bytes 1048576
  74.7 1.1 %constant_dynamic-update-slice_fusion.3 = bf16[2,2048,512]{2,1,0:T(8,128)(2,1)S(1)} fusion(bf16[2,2048,512]{2,1,0:T(8,128)(2,1)S(1)} %constant_dynamic-update-slice_fusion.4, bf16[2,256,512]{2,1,0:T(8,128)(2,1)} %collective-permute-done.2), kind=kLoop, calls=%fused_computation.148 | loop fusion | bytes 1048576
  75.8 1.1 %constant_dynamic-update-slice_fusion.2 = bf16[2,2048,512]{2,1,0:T(8,128)(2,1)S(1)} fusion(bf16[2,2048,512]{2,1,0:T(8,128)(2,1)S(1)} %constant_dynamic-update-slice_fusion.3, bf16[2,256,512]{2,1,0:T(8,128)(2,1)} %collective-permute-done.1), kind=kLoop, calls=%fused_computation.147 | loop fusion | bytes 1048576
  77.1 1.1 %squeeze.8 = bf16[1024,4,128]{2,1,0:T(4,128)(2,1)} reshape(bf16[1,1024,512]{2,1,0:T(8,128)(2,1)S(1)} %get-tuple-element.38) | data formatting | bytes 2097152 | tf_op jit(solution)/shard_map/while/body/eval_jaxpr/reshape;while/body/eval_jaxpr/squeeze | solution.py:147
  78.3 2.4 %select_reduce_fusion = (f32[4,256]{1,0:T(4,128)S(1)}, f32[4,256,1024]{2,1,0:T(8,128)S(1)}) fusion(pred[256,1024]{1,0:T(8,128)(4,1)S(1)} %broadcast_compare_fusion, bf16[1024,4,128]{2,1,0:T(4,128)(2,1)} %squeeze.8, bf16[32,4,8,128]{3,2,1,0:T(8,128)(2,1)} %fusion.17), kind=kOutput, calls=%fused_computation.5 | convolution fusion | flops 271580160 | bytes 5771264 | tf_op jit(solution)/shard_map/while/body/eval_jaxpr/qhd,khd->hqk/dot_general | solution.py:44
  80.7 1.9 %copy-done.1 = f32[4,256,1024]{2,1,0:T(8,128)} copy-done((f32[4,256,1024]{2,1,0:T(8,128)}, f32[4,256,1024]{2,1,0:T(8,128)S(1)}, u32[]{:S(2)}) %copy-start.1) | copy-done | bytes 4194328
  82.6 1.4 %fusion = f32[4,256]{1,0:T(4,128)S(1)} fusion(f32[4,256,1024]{2,1,0:T(8,128)S(1)} %get-tuple-element.107, f32[4,256]{1,0:T(4,128)S(1)} %get-tuple-element.75, pred[256,1024]{1,0:T(8,128)(4,1)S(1)} %broadcast_compare_fusion), kind=kLoop, calls=%fused_computation.6 | loop fusion | flops 4193280 | bytes 4464640 | tf_op jit(solution)/shard_map/while/body/eval_jaxpr/reduce_sum | solution.py:52
  84.5 3.4 %fusion.93 = bf16[256,4,128]{0,2,1:T(8,128)(2,1)S(1)} fusion(bf16[1024,4,128]{0,2,1:T(8,128)(2,1)S(1)} %bitcast.79, f32[4,256,1024]{2,1,0:T(8,128)} %copy-done.1, f32[4,256]{1,0:T(4,128)S(1)} %get-tuple-element.75, pred[256,1024]{1,0:T(8,128)(4,1)S(1)} %broadcast_compare_fusion, f32[256,4]{0,1:T(4,128)S(1)} %bitcast_add_fusion, ...), kind=kOutput, calls=%fused_computation.132 | convolution fusion | flops 273022976 | bytes 5779456 | tf_op jit(solution)/shard_map/while/body/eval_jaxpr/hqk,khd->hqd/dot_general | solution.py:53
  89.5 1.3 %collective-permute-start.3 = (bf16[15,1024]{1,0:T(8,128)(2,1)S(1)}, bf16[15,1024]{1,0:T(8,128)(2,1)S(1)}, u32[]{:S(2)}, u32[]{:S(2)}) collective-permute-start(bf16[15,1024]{1,0:T(8,128)(2,1)S(1)} %get-tuple-element.41), channel_id=1, source_target_pairs={{0,1},{1,2},{2,3},{4,5},{5,6},{6,7},{8,9},{9,10},{10,11},{12,13},{... | collective-permute-start | bytes 92168 | tf_op jit(solution)/shard_map/ppermute | solution.py:19
  90.8 1.3 %collective-permute-start.4 = (bf16[15,1024]{1,0:T(8,128)(2,1)S(1)}, bf16[15,1024]{1,0:T(8,128)(2,1)S(1)}, u32[]{:S(2)}, u32[]{:S(2)}) collective-permute-start(bf16[15,1024]{1,0:T(8,128)(2,1)S(1)} %get-tuple-element.42), channel_id=1, source_target_pairs={{1,0},{2,1},{3,2},{5,4},{6,5},{7,6},{9,8},{10,9},{11,10},{13,12},{... | collective-permute-start | bytes 92168 | tf_op jit(solution)/shard_map/ppermute | solution.py:22
  92.4 4.2 %collective-permute-done.4 = bf16[15,1024]{1,0:T(8,128)(2,1)S(1)} collective-permute-done((bf16[15,1024]{1,0:T(8,128)(2,1)S(1)}, bf16[15,1024]{1,0:T(8,128)(2,1)S(1)}, u32[]{:S(2)}, u32[]{:S(2)}) %collective-permute-start.4) | collective-permute-done | bytes 30752 | tf_op jit(solution)/shard_map/ppermute | solution.py:22
  97.1 8.0 %fusion.22 = bf16[256,1024]{1,0:T(8,128)(2,1)} fusion(bf16[256,1024]{1,0:T(8,128)(2,1)S(1)} %get-tuple-element.109, f32[286,1024]{1,0:T(8,128)S(1)} %maximum_convert_fusion, f32[1024]{0:T(1024)S(1)} %copy-done.37, f32[1024]{0:T(1024)S(1)} %copy-done.38, f32[1024]{0:T(1024)S(1)} %bitcast.92, f32[1024]{0:T(1024)S(1)} %bitcast.93, f32[1024]{0:T(1024)S(1)} %bitcast.95, ...), kind=kLoop, calls=%fused_computation.30 | loop fusion | flops 26476544 | bytes 33697536 | tf_op jit(solution)/shard_map/convert_element_type | solution.py:193
  (138 shorter events, 6.3 us)
Async XLA Ops:
  0.0 88.3 %copy-start = (bf16[512,1024]{1,0:T(8,128)(2,1)S(1)}, bf16[512,1024]{1,0:T(8,128)(2,1)}, u32[]{:S(2)}) copy-start(bf16[512,1024]{1,0:T(8,128)(2,1)} %param.18) | copy-start | bytes 3145732
  2.1 25.1 %copy-start.3 = (bf16[1024,512]{1,0:T(8,128)(2,1)S(1)}, bf16[1024,512]{1,0:T(8,128)(2,1)}, u32[]{:S(2)}) copy-start(bf16[1024,512]{1,0:T(8,128)(2,1)} %param.16) | copy-start | bytes 3145732
  4.8 20.8 %all-to-all-start = ((bf16[4,4,16,1024]{3,2,1,0:T(8,128)(2,1)}), bf16[4,4,16,1024]{3,2,1,0:T(8,128)(2,1)S(1)}, u32[]{:S(2)}, u32[]{:S(2)}) async-start(bf16[4,4,16,1024]{3,2,1,0:T(8,128)(2,1)} %bitcast.1), calls=%async_computation | async-start | bytes 1048576 | tf_op jit(solution)/shard_map/all_to_all | solution.py:117
  13.8 16.4 %copy-start.36 = (pred[16]{0:T(512)(128)(4,1)}, pred[16]{0:T(512)(128)(4,1)S(1)}, u32[]{:S(2)}) copy-start(pred[16]{0:T(512)(128)(4,1)S(1)} %get-tuple-element.24) | copy-start | bytes 52
  30.2 14.9 %collective-permute-start = (bf16[2,256,512]{2,1,0:T(8,128)(2,1)}, bf16[2,256,512]{2,1,0:T(8,128)(2,1)S(1)}, u32[]{:S(2)}, u32[]{:S(2)}) collective-permute-start(bf16[2,256,512]{2,1,0:T(8,128)(2,1)} %pad_maximum_fusion), channel_id=1, source_target_pairs={{0,1},{1,2},{2,3},{3,0},{4,5},{5,6},{6,7},{7,4},{8,9},{9,10},{10,1... | collective-permute-start | bytes 1572872 | tf_op jit(solution)/shard_map/ppermute | solution.py:154
  45.2 14.0 %collective-permute-start.1 = (bf16[2,256,512]{2,1,0:T(8,128)(2,1)S(1)}, bf16[2,256,512]{2,1,0:T(8,128)(2,1)}, u32[]{:S(2)}, u32[]{:S(2)}) collective-permute-start(bf16[2,256,512]{2,1,0:T(8,128)(2,1)S(1)} %collective-permute-done), channel_id=1, source_target_pairs={{0,1},{1,2},{2,3},{3,0},{4,5},{5,6},{6,7},{7,4},{8,9},{9,10},{10,1... | collective-permute-start | bytes 1572872 | tf_op jit(solution)/shard_map/ppermute | solution.py:154
  45.8 13.4 %copy-start.34 = (s32[256]{0:T(256)}, s32[256]{0:T(256)S(1)}, u32[]{:S(2)}) copy-start(s32[256]{0:T(256)S(1)} %get-tuple-element.23) | copy-start | bytes 3076
  59.1 13.3 %collective-permute-start.2 = (bf16[2,256,512]{2,1,0:T(8,128)(2,1)}, bf16[2,256,512]{2,1,0:T(8,128)(2,1)}, u32[]{:S(2)}, u32[]{:S(2)}) collective-permute-start(bf16[2,256,512]{2,1,0:T(8,128)(2,1)} %collective-permute-done.1), channel_id=1, source_target_pairs={{0,1},{1,2},{2,3},{3,0},{4,5},{5,6},{6,7},{7,4},{8,9},{9,10},{10,1... | collective-permute-start | bytes 1572872 | tf_op jit(solution)/shard_map/ppermute | solution.py:154
  88.0 8.8 %copy-start.5 = (f32[1,1024]{1,0:T(1,128)S(1)}, f32[1,1024]{1,0:T(1,128)}, u32[]{:S(2)}) copy-start(f32[1,1024]{1,0:T(1,128)} %get-tuple-element.64) | copy-start | bytes 12292
  88.0 8.8 %copy-start.6 = (f32[1,1024]{1,0:T(1,128)S(1)}, f32[1,1024]{1,0:T(1,128)}, u32[]{:S(2)}) copy-start(f32[1,1024]{1,0:T(1,128)} %get-tuple-element.65) | copy-start | bytes 12292
  88.0 8.8 %copy-start.7 = (f32[1,1024]{1,0:T(1,128)S(1)}, f32[1,1024]{1,0:T(1,128)}, u32[]{:S(2)}) copy-start(f32[1,1024]{1,0:T(1,128)} %get-tuple-element.66) | copy-start | bytes 12292
  88.0 8.8 %copy-start.8 = (f32[1,1024]{1,0:T(1,128)S(1)}, f32[1,1024]{1,0:T(1,128)}, u32[]{:S(2)}) copy-start(f32[1,1024]{1,0:T(1,128)} %get-tuple-element.67) | copy-start | bytes 12292
  88.0 8.8 %copy-start.9 = (f32[1,1024]{1,0:T(1,128)S(1)}, f32[1,1024]{1,0:T(1,128)}, u32[]{:S(2)}) copy-start(f32[1,1024]{1,0:T(1,128)} %get-tuple-element.68) | copy-start | bytes 12292
  88.0 8.8 %copy-start.10 = (f32[1,1024]{1,0:T(1,128)S(1)}, f32[1,1024]{1,0:T(1,128)}, u32[]{:S(2)}) copy-start(f32[1,1024]{1,0:T(1,128)} %get-tuple-element.69) | copy-start | bytes 12292
  88.0 8.8 %copy-start.11 = (f32[1,1024]{1,0:T(1,128)S(1)}, f32[1,1024]{1,0:T(1,128)}, u32[]{:S(2)}) copy-start(f32[1,1024]{1,0:T(1,128)} %get-tuple-element.70) | copy-start | bytes 12292
  88.0 8.8 %copy-start.12 = (f32[1,1024]{1,0:T(1,128)S(1)}, f32[1,1024]{1,0:T(1,128)}, u32[]{:S(2)}) copy-start(f32[1,1024]{1,0:T(1,128)} %get-tuple-element.71) | copy-start | bytes 12292
  88.0 8.8 %copy-start.13 = (f32[1,1024]{1,0:T(1,128)S(1)}, f32[1,1024]{1,0:T(1,128)}, u32[]{:S(2)}) copy-start(f32[1,1024]{1,0:T(1,128)} %get-tuple-element.72) | copy-start | bytes 12292
  88.0 8.8 %copy-start.14 = (f32[1,1024]{1,0:T(1,128)S(1)}, f32[1,1024]{1,0:T(1,128)}, u32[]{:S(2)}) copy-start(f32[1,1024]{1,0:T(1,128)} %get-tuple-element.73) | copy-start | bytes 12292
  88.1 8.8 %copy-start.15 = (f32[1,1024]{1,0:T(1,128)S(1)}, f32[1,1024]{1,0:T(1,128)}, u32[]{:S(2)}) copy-start(f32[1,1024]{1,0:T(1,128)} %get-tuple-element.43) | copy-start | bytes 12292
  88.1 8.8 %copy-start.16 = (f32[1,1024]{1,0:T(1,128)S(1)}, f32[1,1024]{1,0:T(1,128)}, u32[]{:S(2)}) copy-start(f32[1,1024]{1,0:T(1,128)} %get-tuple-element.44) | copy-start | bytes 12292
  88.1 8.8 %copy-start.17 = (f32[1,1024]{1,0:T(1,128)S(1)}, f32[1,1024]{1,0:T(1,128)}, u32[]{:S(2)}) copy-start(f32[1,1024]{1,0:T(1,128)} %get-tuple-element.45) | copy-start | bytes 12292
  88.1 8.8 %copy-start.18 = (f32[1,1024]{1,0:T(1,128)S(1)}, f32[1,1024]{1,0:T(1,128)}, u32[]{:S(2)}) copy-start(f32[1,1024]{1,0:T(1,128)} %get-tuple-element.46) | copy-start | bytes 12292
  88.1 8.8 %copy-start.19 = (f32[1,1024]{1,0:T(1,128)S(1)}, f32[1,1024]{1,0:T(1,128)}, u32[]{:S(2)}) copy-start(f32[1,1024]{1,0:T(1,128)} %get-tuple-element.47) | copy-start | bytes 12292
  88.1 8.8 %copy-start.20 = (f32[1,1024]{1,0:T(1,128)S(1)}, f32[1,1024]{1,0:T(1,128)}, u32[]{:S(2)}) copy-start(f32[1,1024]{1,0:T(1,128)} %get-tuple-element.48) | copy-start | bytes 12292
  88.1 8.8 %copy-start.21 = (f32[1,1024]{1,0:T(1,128)S(1)}, f32[1,1024]{1,0:T(1,128)}, u32[]{:S(2)}) copy-start(f32[1,1024]{1,0:T(1,128)} %get-tuple-element.49) | copy-start | bytes 12292
  88.1 8.8 %copy-start.22 = (f32[1,1024]{1,0:T(1,128)S(1)}, f32[1,1024]{1,0:T(1,128)}, u32[]{:S(2)}) copy-start(f32[1,1024]{1,0:T(1,128)} %get-tuple-element.50) | copy-start | bytes 12292
  88.1 8.8 %copy-start.23 = (f32[1,1024]{1,0:T(1,128)S(1)}, f32[1,1024]{1,0:T(1,128)}, u32[]{:S(2)}) copy-start(f32[1,1024]{1,0:T(1,128)} %get-tuple-element.51) | copy-start | bytes 12292
  88.2 8.8 %copy-start.24 = (f32[1,1024]{1,0:T(1,128)S(1)}, f32[1,1024]{1,0:T(1,128)}, u32[]{:S(2)}) copy-start(f32[1,1024]{1,0:T(1,128)} %get-tuple-element.52) | copy-start | bytes 12292
  88.2 8.8 %copy-start.25 = (f32[1,1024]{1,0:T(1,128)S(1)}, f32[1,1024]{1,0:T(1,128)}, u32[]{:S(2)}) copy-start(f32[1,1024]{1,0:T(1,128)} %get-tuple-element.53) | copy-start | bytes 12292
  88.2 8.8 %copy-start.26 = (f32[1,1024]{1,0:T(1,128)S(1)}, f32[1,1024]{1,0:T(1,128)}, u32[]{:S(2)}) copy-start(f32[1,1024]{1,0:T(1,128)} %get-tuple-element.54) | copy-start | bytes 12292
  89.5 2.9 %collective-permute-start.3 = (bf16[15,1024]{1,0:T(8,128)(2,1)S(1)}, bf16[15,1024]{1,0:T(8,128)(2,1)S(1)}, u32[]{:S(2)}, u32[]{:S(2)}) collective-permute-start(bf16[15,1024]{1,0:T(8,128)(2,1)S(1)} %get-tuple-element.41), channel_id=1, source_target_pairs={{0,1},{1,2},{2,3},{4,5},{5,6},{6,7},{8,9},{9,10},{10,11},{12,13},{... | collective-permute-start | bytes 92168 | tf_op jit(solution)/shard_map/ppermute | solution.py:19
  90.8 5.8 %collective-permute-start.4 = (bf16[15,1024]{1,0:T(8,128)(2,1)S(1)}, bf16[15,1024]{1,0:T(8,128)(2,1)S(1)}, u32[]{:S(2)}, u32[]{:S(2)}) collective-permute-start(bf16[15,1024]{1,0:T(8,128)(2,1)S(1)} %get-tuple-element.42), channel_id=1, source_target_pairs={{1,0},{2,1},{3,2},{5,4},{6,5},{7,6},{9,8},{10,9},{11,10},{13,12},{... | collective-permute-start | bytes 92168 | tf_op jit(solution)/shard_map/ppermute | solution.py:22
  (19 other events, 149.5 us)
